TPU v7x, 512 devices: a whole 4x4x16 slice. The times are simulated.
512 devices in a mesh: dp: 32 (over y_hi, z), rep: 16 (over x, y_lo, core).
Axes of the slice: x: 4, y: 4 (y_hi: 2, y_lo: 2; y = y_hi * 2 + y_lo), z: 16, core: 2. Of those that a mesh axis runs over, the one named last changes fastest.
Arguments:
- mentions: bfloat16 [65536, 1024], P(('dp', 'rep')), may hold values from -48 to 48
- entity_states: bfloat16 [65536, 1024], P(('dp', 'rep')), may hold values from -8 to 8
- head: bfloat16 [1024, 1024], P('dp'), may hold values from -4 to 4
Outputs:
- pair_loss: float32 [65536], P(('dp', 'rep'))
- mention_grad: bfloat16 [65536, 1024], P(('dp', 'rep'))
- state_grad: bfloat16 [65536, 1024], P(('dp', 'rep'))
All inputs are finite; a program needn't handle non-finite values.
Results may differ from a plain program's by a relative error of at most 0.0073.
Values may be sent and summed in bfloat16 or wider, within the bound.
A program may use at most 64 MiB of HBM per device.

v0:
```python
import math

import jax
import jax.numpy as jnp
from jax import lax
from jax.sharding import Mesh
from jax.sharding import PartitionSpec as P

DP = ("dp_0", "dp_1")
REP = ("rep_0", "rep_1", "rep_2")
DP_REP = ("dp_0", "dp_1", "rep_0", "rep_1", "rep_2")


def in_order(blocks, dim):
    lengths = list(blocks.shape[1:])
    lengths[dim] *= blocks.shape[0]
    return jnp.moveaxis(blocks, 0, dim).reshape(lengths)


def stacked_from(array, axes, sequence):
    blocks = array
    for k in sequence:
        blocks = lax.all_gather(blocks, axes[k])
    done = sequence[::-1]
    back = [done.index(k) for k in range(len(axes))]
    blocks = blocks.transpose(*back, *range(len(axes), blocks.ndim))
    return blocks.reshape(-1, *array.shape)


def gather_axes(array, axes, sequence, dim):
    return in_order(stacked_from(array, axes, sequence), dim)


def sent_to_all(array, axis):
    count = lax.axis_size(axis)
    return lax.all_to_all(
        jnp.broadcast_to(array[None], (count, *array.shape)), axis, 0, 0, tiled=True
    )


def whole_of(array, axes, dim):
    far, near = axes
    leading = sent_to_all(array, far)
    blocks = jnp.swapaxes(sent_to_all(leading, near), 0, 1)
    return in_order(blocks.reshape(-1, *array.shape), dim)


def collect(array, axis, dim):
    return in_order(sent_to_all(array, axis), dim)


def local(mentions, entity_states, head):
    row_count, feature_count = mentions.shape
    scale_factor = 3.0 / math.sqrt(feature_count)
    contract = (((1,), (1,)), ((), ()))

    def score(left_rows, right_rows):
        return (
            lax.dot_general(left_rows, right_rows, contract, preferred_element_type=jnp.float32)
            * scale_factor
        )

    weights = gather_axes(head, DP, (0, 1), 0)
    projected = jnp.dot(entity_states, weights, preferred_element_type=jnp.float32).astype(
        jnp.bfloat16
    )
    matched = (
        jnp.einsum("rd,rd->r", mentions, projected, preferred_element_type=jnp.float32)
        * scale_factor
    )
    gathered = whole_of(projected, (("rep_0", "rep_1"), "rep_2"), 0)
    scores = score(mentions, gathered)
    row_max = jnp.max(scores, axis=1)
    log_total = row_max + jnp.log(jnp.sum(jnp.exp(scores - row_max[:, None]), axis=1))
    chances = jnp.exp(scores - log_total[:, None]).astype(jnp.bfloat16)
    weighted = jnp.dot(chances, gathered, preferred_element_type=jnp.float32)
    pair_loss = log_total - matched
    mention_grad = (scale_factor * (weighted - projected.astype(jnp.float32))).astype(jnp.bfloat16)
    totals = collect(log_total, REP, 0)
    portion = whole_of(mentions, (("rep_0", "rep_1"), "rep_2"), 0)
    scores = score(portion, projected)
    chances = jnp.exp(scores - totals[:, None]).astype(jnp.bfloat16)
    summed = lax.dot_general(
        chances, portion, (((0,), (0,)), ((), ())), preferred_element_type=jnp.float32
    )
    proj_grad = (scale_factor * (summed - mentions.astype(jnp.float32))).astype(jnp.bfloat16)
    state_grad = lax.dot_general(
        proj_grad, weights, contract, preferred_element_type=jnp.float32
    ).astype(jnp.bfloat16)
    return (pair_loss, mention_grad, state_grad)


def solution(mesh):
    torus = Mesh(mesh.devices.reshape(2, 16, 4, 2, 2), ("dp_0", "dp_1", "rep_0", "rep_1", "rep_2"))
    in_specs = (P(DP_REP, None), P(DP_REP, None), P(DP, None))
    out_specs = (P(DP_REP), P(DP_REP, None), P(DP_REP, None))
    return jax.shard_map(local, mesh=torus, in_specs=in_specs, out_specs=out_specs, check_vma=False)
```

profile of v0, /device:TPU:1, one launch (start us, length us, event | category | flops | bytes accessed | tf_op | source)
XLA Modules:
  0.0 161.6 jit_solution(10202869379733181283)
XLA Ops:
  7.2 0.0 copy-start
  7.2 0.0 all-gather.4.cloned.1.call-start
  7.2 7.9 %all-gather = bf16[64,1024]{1,0:T(8,128)(2,1)} all-gather(bf16[32,1024]{1,0:T(8,128)(2,1)} %param.5), channel_id=2, replica_groups=mesh['dp_0'=2,'dp_1'=16,'rep_0'=4,'rep_1'=2,'rep_2'=2] {'dp_0'}, dimensions={0}, use_global_device_ids=true | all-gather | bytes 196608 | tf_op jit(solution)/shard_map/all_gather | solution.py:23
  15.2 0.0 all-gather.4.cloned.1.call-update
  15.2 1.2 broadcast_in_dim.12
  16.4 26.2 %all_to_all.26 = bf16[8,128,1024]{2,1,0:T(8,128)(2,1)S(1)} all-to-all(bf16[8,128,1024]{2,1,0:T(8,128)(2,1)S(1)} %broadcast_in_dim.12), channel_id=1, replica_groups=mesh['dp_0'=2,'dp_1'=16,'rep_0'=4,'rep_1'=2,'rep_2'=2] {'rep_0','rep_1'}, dimensions={0} | all-to-all | bytes 4194304 | tf_op jit(solution)/shard_map/all_to_all | solution.py:36
  42.6 2.5 %broadcast_in_dim.13 = bf16[2,8,128,1024]{3,2,1,0:T(8,128)(2,1)} broadcast(bf16[8,128,1024]{2,1,0:T(8,128)(2,1)S(1)} %all_to_all.26), dimensions={1,2,3} | broadcast | bytes 6291456 | tf_op jit(solution)/shard_map/broadcast_in_dim | solution.py:37
  45.2 10.8 %all-to-all-start.3 = ((bf16[2,8,128,1024]{3,2,1,0:T(8,128)(2,1)}), bf16[2,8,128,1024]{3,2,1,0:T(8,128)(2,1)}, u32[]{:S(2)}, u32[]{:S(2)}) async-start(bf16[2,8,128,1024]{3,2,1,0:T(8,128)(2,1)} %broadcast_in_dim.13), calls=%async_computation.3 | async-start | bytes 8388608 | tf_op jit(solution)/shard_map/all_to_all | solution.py:36
  56.0 0.0 copy-start.2
  56.0 27.4 %all-gather.4.cloned.1.call-done = bf16[32,32,1024]{2,1,0:T(8,128)(2,1)} async-done(((bf16[2,32,1024]{2,1,0:T(8,128)(2,1)}), bf16[32,32,1024]{2,1,0:T(8,128)(2,1)}) %all-gather.4.cloned.1.call-update) | async-done | bytes 2097168 | tf_op jit(solution)/shard_map/all_gather | solution.py:23
  83.4 1.9 %copy.7 = bf16[2,16,32,1024]{3,2,1,0:T(8,128)(2,1)S(1)} copy(bf16[2,16,32,1024]{3,2,0,1:T(8,128)(2,1)} %bitcast.28) | data formatting | bytes 4194304 | tf_op jit(solution)/shard_map/transpose | solution.py:26
  85.2 0.0 copy-done
  85.2 0.0 copy-done.2
  85.2 0.5 fusion.8
  85.8 0.0 copy-start.5
  85.8 0.0 all-to-all-done.3
  85.8 1.6 broadcast_in_dim.10
  87.4 5.0 %all-to-all-start = ((bf16[8,128,1024]{2,1,0:T(8,128)(2,1)}), bf16[8,128,1024]{2,1,0:T(8,128)(2,1)}, u32[]{:S(2)}, u32[]{:S(2)}) async-start(bf16[8,128,1024]{2,1,0:T(8,128)(2,1)} %broadcast_in_dim.10), calls=%async_computation | async-start | bytes 4194304 | tf_op jit(solution)/shard_map/all_to_all | solution.py:36
  92.4 4.7 %copy.9 = bf16[2,8,128,1024]{3,2,0,1:T(8,128)(2,1)} copy(bf16[2,8,128,1024]{3,2,1,0:T(8,128)(2,1)} %all-to-all-done.3) | data formatting | bytes 8388608 | tf_op jit(solution)/shard_map/all_to_all | solution.py:36
  97.1 0.0 copy-done.5
  97.1 16.4 %all-to-all-done = bf16[8,128,1024]{2,1,0:T(8,128)(2,1)} async-done(((bf16[8,128,1024]{2,1,0:T(8,128)(2,1)}), bf16[8,128,1024]{2,1,0:T(8,128)(2,1)}, u32[]{:S(2)}, u32[]{:S(2)}) %all-to-all-start) | async-done | bytes 2097184 | tf_op jit(solution)/shard_map/all_to_all | solution.py:36
  113.6 2.1 %broadcast_in_dim.11 = bf16[2,8,128,1024]{3,2,1,0:T(8,128)(2,1)S(1)} broadcast(bf16[8,128,1024]{2,1,0:T(8,128)(2,1)} %all-to-all-done), dimensions={1,2,3} | broadcast | bytes 6291456 | tf_op jit(solution)/shard_map/broadcast_in_dim | solution.py:37
  115.7 15.3 %all_to_all.27 = bf16[2,8,128,1024]{3,2,1,0:T(8,128)(2,1)S(1)} all-to-all(bf16[2,8,128,1024]{3,2,1,0:T(8,128)(2,1)S(1)} %broadcast_in_dim.11), channel_id=1, replica_groups=mesh['dp_0'=2,'dp_1'=16,'rep_0'=4,'rep_1'=2,'rep_2'=2] {'rep_2'}, dimensions={0} | all-to-all | bytes 8388608 | tf_op jit(solution)/shard_map/all_to_all | solution.py:36
  131.0 0.0 copy-start.3
  131.0 0.6 copy.8
  131.6 0.0 copy-start.1
  131.6 2.0 %copy-done.1 = bf16[2,8,128,1024]{3,2,0,1:T(8,128)(2,1)} copy-done((bf16[2,8,128,1024]{3,2,0,1:T(8,128)(2,1)}, bf16[2,8,128,1024]{3,2,0,1:T(8,128)(2,1)S(1)}, u32[]{:S(2)}) %copy-start.1) | copy-done | bytes 4194328
  133.6 0.0 copy-done.3
  133.6 1.3 fusion.12
  134.9 0.3 exponential_reduce_fusion
  135.1 0.5 multiply_subtract_fusion
  135.7 0.6 broadcast_in_dim.14
  136.3 4.8 %all-to-all-start.4 = ((f32[16,1,128]{2,1,0:T(1,128)}), f32[16,1,128]{2,1,0:T(1,128)S(1)}, u32[]{:S(2)}, u32[]{:S(2)}) async-start(f32[16,1,128]{2,1,0:T(1,128)} %broadcast_in_dim.14), calls=%async_computation.4 | async-start | bytes 16384 | tf_op jit(solution)/shard_map/all_to_all | solution.py:36
  141.1 3.7 %fusion.6 = bf16[128,1024]{1,0:T(8,128)(2,1)} fusion(bf16[2048,1024]{1,0:T(8,128)(2,1)} %bitcast.23, bf16[128,1024]{1,0:T(8,128)(2,1)} %copy-done.5, f32[2048,128]{1,0:T(8,128)S(1)} %get-tuple-element.8, f32[128]{0:T(128)S(1)} %get-tuple-element.4), kind=kOutput, calls=%fused_computation.10 | convolution fusion | flops 537919488 | bytes 5767680 | tf_op jit(solution)/shard_map/dot_general | solution.py:76
  144.8 0.0 copy-start.4
  144.8 1.8 %all-to-all-done.4 = f32[16,1,128]{2,1,0:T(1,128)S(1)} async-done(((f32[16,1,128]{2,1,0:T(1,128)}), f32[16,1,128]{2,1,0:T(1,128)S(1)}, u32[]{:S(2)}, u32[]{:S(2)}) %all-to-all-start.4) | async-done | bytes 8224 | tf_op jit(solution)/shard_map/all_to_all | solution.py:36
  146.6 3.8 %fusion.2 = bf16[128,2048]{1,0:T(8,128)(2,1)S(1)} fusion(bf16[128,1024]{1,0:T(8,128)(2,1)} %copy-done.5, bf16[2048,1024]{1,0:T(8,128)(2,1)} %bitcast.24, f32[2048]{0:T(1024)S(1)} %bitcast.30), kind=kOutput, calls=%fused_computation.4 | convolution fusion | flops 537657344 | bytes 4988928 | tf_op jit(solution)/shard_map/dot_general | solution.py:59
  150.4 0.0 copy-done.4
  150.4 4.3 %convolution_convert_fusion = bf16[128,1024]{1,0:T(8,128)(2,1)} fusion(bf16[1024,1024]{1,0:T(8,128)(2,1)S(1)} %bitcast.27, bf16[128,2048]{1,0:T(8,128)(2,1)S(1)} %fusion.2, bf16[2048,1024]{1,0:T(8,128)(2,1)} %bitcast.25, bf16[128,1024]{1,0:T(8,128)(2,1)S(1)} %copy-done.4), kind=kOutput, calls=%fused_computation.11 | convolution fusion | flops 805961728 | bytes 7340032 | tf_op jit(solution)/shard_map/dot_general | solution.py:87
Async XLA Ops:
  7.2 78.1 %copy-start = (bf16[128,1024]{1,0:T(8,128)(2,1)S(1)}, bf16[128,1024]{1,0:T(8,128)(2,1)}, u32[]{:S(2)}) copy-start(bf16[128,1024]{1,0:T(8,128)(2,1)} %param.4) | copy-start | bytes 786436
  7.2 76.2 %all-gather.4.cloned.1.call-start = ((), (), s32[]{:S(2)}) async-start(), calls=%async_computation.5 | async-start | bytes 2228224 | tf_op jit(solution)/shard_map/all_gather | solution.py:23
  45.2 40.6 %all-to-all-start.3 = ((bf16[2,8,128,1024]{3,2,1,0:T(8,128)(2,1)}), bf16[2,8,128,1024]{3,2,1,0:T(8,128)(2,1)}, u32[]{:S(2)}, u32[]{:S(2)}) async-start(bf16[2,8,128,1024]{3,2,1,0:T(8,128)(2,1)} %broadcast_in_dim.13), calls=%async_computation.3 | async-start | bytes 8388608 | tf_op jit(solution)/shard_map/all_to_all | solution.py:36
  56.0 29.2 %copy-start.2 = (bf16[128,1024]{1,0:T(8,128)(2,1)S(1)}, bf16[128,1024]{1,0:T(8,128)(2,1)}, u32[]{:S(2)}) copy-start(bf16[128,1024]{1,0:T(8,128)(2,1)} %param.3) | copy-start | bytes 786436
  85.8 11.4 %copy-start.5 = (bf16[128,1024]{1,0:T(8,128)(2,1)}, bf16[128,1024]{1,0:T(8,128)(2,1)S(1)}, u32[]{:S(2)}) copy-start(bf16[128,1024]{1,0:T(8,128)(2,1)S(1)} %get-tuple-element.6) | copy-start | bytes 786436
  87.4 26.2 %all-to-all-start = ((bf16[8,128,1024]{2,1,0:T(8,128)(2,1)}), bf16[8,128,1024]{2,1,0:T(8,128)(2,1)}, u32[]{:S(2)}, u32[]{:S(2)}) async-start(bf16[8,128,1024]{2,1,0:T(8,128)(2,1)} %broadcast_in_dim.10), calls=%async_computation | async-start | bytes 4194304 | tf_op jit(solution)/shard_map/all_to_all | solution.py:36
  131.0 2.6 %copy-start.3 = (bf16[128,1024]{1,0:T(8,128)(2,1)S(1)}, bf16[128,1024]{1,0:T(8,128)(2,1)}, u32[]{:S(2)}) copy-start(bf16[128,1024]{1,0:T(8,128)(2,1)} %param.3) | copy-start | bytes 786436
  131.6 2.0 %copy-start.1 = (bf16[2,8,128,1024]{3,2,0,1:T(8,128)(2,1)}, bf16[2,8,128,1024]{3,2,0,1:T(8,128)(2,1)S(1)}, u32[]{:S(2)}) copy-start(bf16[2,8,128,1024]{3,2,0,1:T(8,128)(2,1)S(1)} %copy.8) | copy-start | bytes 12582916
  136.3 10.3 %all-to-all-start.4 = ((f32[16,1,128]{2,1,0:T(1,128)}), f32[16,1,128]{2,1,0:T(1,128)S(1)}, u32[]{:S(2)}, u32[]{:S(2)}) async-start(f32[16,1,128]{2,1,0:T(1,128)} %broadcast_in_dim.14), calls=%async_computation.4 | async-start | bytes 16384 | tf_op jit(solution)/shard_map/all_to_all | solution.py:36
  144.8 5.7 %copy-start.4 = (bf16[128,1024]{1,0:T(8,128)(2,1)S(1)}, bf16[128,1024]{1,0:T(8,128)(2,1)}, u32[]{:S(2)}) copy-start(bf16[128,1024]{1,0:T(8,128)(2,1)} %param.3) | copy-start | bytes 786436
Sparse Core Ops, SparseCore 0:
  15.3 68.0 all-gather.3
where the time goes:
time: 162 us
  blocking collectives  49.4 us (30%)
  waiting for transfers between devices  45.6 us (28%)
  starting transfers between devices  20.7 us (13%)
  local copies, waits for them, and re-layouts  17.2 us (11%)
  between operations  14.1 us (9%)
  matrix products  13.6 us (8%)
    all_to_all x2, blocking collectives, sent_to_all(): lax.all_to_all(jnp.broadcast_to(array[None], (count, *array.shape)), axis...  41.5 us
    all_gather x1, waiting for transfers between devices, stacked_from(): blocks = lax.all_gather(blocks, axes[k])  27.4 us
    all_to_all x3, starting transfers between devices, sent_to_all(): lax.all_to_all(jnp.broadcast_to(array[None], (count, *array.shape)), axis...  20.7 us
    all_to_all x3, waiting for transfers between devices, sent_to_all(): lax.all_to_all(jnp.broadcast_to(array[None], (count, *array.shape)), axis...  18.3 us
    broadcast_in_dim x5, local copies, waits for them, and re-layouts, sent_to_all(): jnp.broadcast_to(array[None], (count, *array.shape))  8.05 us
    all_gather x1, blocking collectives, stacked_from(): blocks = lax.all_gather(blocks, axes[k])  7.94 us
    all_to_all x2, local copies, waits for them, and re-layouts, sent_to_all(): lax.all_to_all(jnp.broadcast_to(array[None], (count, *array.shape)), axis...  5.33 us
    dot_general x2, matrix products, score(): lax.dot_general(left_rows, right_rows, contract, preferred_element_type=j...  5.12 us
  transfers between devices with their start and end apart: 4, of which 3 were waited for; matrix products, arithmetic and copies ran while one was open for 9% of the time, Pallas kernels for 0%

commit v1 on v0

v1 whole, which is shorter than its diff:
```python
import functools
import math

import jax
import jax.numpy as jnp
from jax import lax
from jax.experimental import pallas as pl
from jax.experimental.pallas import tpu as pltpu
from jax.sharding import Mesh
from jax.sharding import PartitionSpec as P

DP_REP = ("dp_0", "dp_1", "rep_0", "rep_1", "rep_2")
MESH = pl.DeviceIdType.MESH
NX, NY, NC = 4, 2, 2
RANKS = NX * NY * NC
CHUNK = 256
NT = (((1,), (1,)), ((), ()))


def kernel(
    nz, scale,
    m_ref, e_ref, h_ref,
    loss_ref, mg_ref, sg_ref,
    m_all, p_all, h_all, e_v, acc, st, ct, lse, lt, dp, out_v,
    local_sem, m_recv, m_sib, p_recv, p_sib, hz_recv, hy_recv, h_sib, st_recv,
    m_send, p_send, h_send, st_send, out_sem,
):
    rows, width = m_ref.shape
    half = rows // 2
    shard = h_ref.shape[0]
    part = shard // NC
    group = rows * RANKS
    yh, z = lax.axis_index("dp_0"), lax.axis_index("dp_1")
    x, y, c = lax.axis_index("rep_0"), lax.axis_index("rep_1"), lax.axis_index("rep_2")
    xa, xb, x2 = lax.rem(x + 1 + 2 * c, NX), lax.rem(x + 3 - 2 * c, NX), lax.rem(x + 2, NX)
    yo, co = 1 - y, 1 - c
    rank = x * 4 + y * 2 + c
    ahead, behind, across, sibling = {"rep_0": xa}, {"rep_0": xb}, {"rep_1": yo}, {"rep_2": co}
    up, down = {"dp_1": lax.rem(z + 1, nz)}, {"dp_1": lax.rem(z + nz - 1, nz)}
    partner = {"dp_0": 1 - yh, "rep_1": yo}

    def peer(k):
        return {
            "rep_0": lax.rem(x + k // 4, NX),
            "rep_1": lax.rem(y + (k // 2) % 2, NY),
            "rep_2": lax.rem(c + k % 2, NC),
        }

    barrier = pltpu.get_barrier_semaphore()
    for device in [up, down, partner] + [peer(k) for k in range(1, RANKS)]:
        pl.semaphore_signal(barrier, inc=1, device_id=device, device_id_type=MESH)
    own = pl.ds(pl.multiple_of(rank * rows, rows), rows)
    own_shard = pl.ds(pl.multiple_of((yh * nz + z) * shard, shard), shard)
    fills = [
        pltpu.make_async_copy(m_ref, m_all.at[own], local_sem.at[0]),
        pltpu.make_async_copy(e_ref, e_v, local_sem.at[1]),
        pltpu.make_async_copy(h_ref, h_all.at[own_shard], local_sem.at[2]),
    ]
    for fill in fills:
        fill.start()
    pl.semaphore_wait(barrier, RANKS + 2)

    def copy(src, dst, send_sem, recv_sem, device):
        return pltpu.make_async_remote_copy(
            src_ref=src, dst_ref=dst, send_sem=send_sem, recv_sem=recv_sem,
            device_id=device, device_id_type=MESH,
        )

    def place(cx, cy, core, piece):
        return pl.ds(pl.multiple_of((cx * 4 + cy * 2 + core) * rows + piece * half, half), half)

    def index(cx, cy, piece):
        return piece * (NX * NY) + cx * NY + cy

    def spread(array, send_sem, recv, sib, each_sib, source=None):
        def src(cx, cy, piece):
            if source is not None:
                return source.at[pl.ds(piece * half, half)]
            return array.at[place(cx, cy, c, piece)]

        def to(device, cx, cy, piece):
            copy(
                src(cx, cy, piece), array.at[place(cx, cy, c, piece)],
                send_sem, recv.at[index(cx, cy, piece)], device,
            ).start()

        def to_sib(cx, cy, piece):
            copy(
                src(cx, cy, piece), array.at[place(cx, cy, c, piece)],
                send_sem, sib.at[index(cx, cy, piece)] if each_sib else sib, sibling,
            ).start()

        def got(cx, cy, piece):
            here = array.at[place(cx, cy, c, piece)]
            copy(here, here, send_sem, recv.at[index(cx, cy, piece)], sibling).wait_recv()

        return to, to_sib, got

    A, B = 0, 1

    def relays(array, send_sem, recv, sib, each_sib):
        to, to_sib, got = spread(array, send_sem, recv, sib, each_sib)

        def step(cx, cy, piece, *devices):
            got(cx, cy, piece)
            for device in devices:
                to(device, cx, cy, piece)
            to_sib(cx, cy, piece)

        def one():
            step(xb, y, A, ahead, across)
            step(x, yo, B, ahead, behind)
            step(xa, y, A, across)

        def two():
            step(x, yo, A)
            step(xa, y, B, behind)
            step(xb, y, B)

        def three():
            step(x2, y, A, across)
            step(xb, yo, B, ahead)
            step(xb, yo, A)
            step(xa, yo, A)
            step(xa, yo, B)

        def four():
            step(x2, y, B)
            step(x2, yo, A)
            step(x2, yo, B)

        return one, two, three, four

    def h_place(cy, cz):
        return pl.ds(pl.multiple_of((cy * nz + cz) * shard + c * part, part), part)

    def h_to(device, recv, cy, cz, source=None):
        here = h_all.at[h_place(cy, cz)]
        src = here if source is None else source.at[pl.ds(pl.multiple_of(c * part, part), part)]
        copy(src, here, h_send, recv, device).start()

    def h_got(recv, cy, cz):
        here = h_all.at[h_place(cy, cz)]
        copy(here, here, h_send, recv, sibling).wait_recv()

    h_to(up, hz_recv.at[z], yh, z, h_ref)
    h_to(down, hz_recv.at[z], yh, z, h_ref)
    h_to(partner, hy_recv.at[z], yh, z, h_ref)
    to, to_sib, _ = spread(m_all, m_send, m_recv, m_sib, False, m_ref)
    to(across, x, y, B)
    to(ahead, x, y, A)
    to(behind, x, y, A)
    to(across, x, y, A)
    to(ahead, x, y, B)
    to(behind, x, y, B)
    to_sib(x, y, A)
    to_sib(x, y, B)
    m_one, m_two, m_three, m_four = relays(m_all, m_send, m_recv, m_sib, False)

    ups = nz // 2
    downs = nz - 1 - ups

    def crossed(cz):
        h_got(hy_recv.at[cz], 1 - yh, cz)
        h_to(sibling, h_sib.at[1], 1 - yh, cz)

    order = []
    order.append(z)
    for step in range(ups):
        cz = lax.rem(z + nz - 1 - step, nz)
        h_got(hz_recv.at[cz], yh, cz)
        if step < ups - 1:
            h_to(up, hz_recv.at[cz], yh, cz)
        h_to(partner, hy_recv.at[cz], yh, cz)
        h_to(sibling, h_sib.at[0], yh, cz)
        order.append(cz)
        if step < downs:
            cz = lax.rem(z + 1 + step, nz)
            h_got(hz_recv.at[cz], yh, cz)
            if step < downs - 1:
                h_to(down, hz_recv.at[cz], yh, cz)
            h_to(partner, hy_recv.at[cz], yh, cz)
            h_to(sibling, h_sib.at[0], yh, cz)
            order.append(cz)
        if step == 2:
            m_one()
        if step == 4:
            m_two()
        if step == 6:
            m_three()
        if step >= 2:
            for cz in order[2 * step - 4 : 2 * step - 2]:
                crossed(cz)
    for cz in order[2 * ups - 4 :]:
        crossed(cz)
    for fill in fills:
        fill.wait()

    def all_of(ref, count, send_sem, recv_sem):
        view = ref.at[pl.ds(0, count)]
        return copy(view, view, send_sem, recv_sem, sibling)

    def columns(n):
        return pl.ds(pl.multiple_of(n * CHUNK, CHUNK), CHUNK)

    def project(cy, first):
        side = nz * shard
        at = pl.ds(pl.multiple_of(cy * side, side), side)

        @pl.loop(0, width // CHUNK)
        def _(n):
            term = jnp.dot(e_v[:, at], h_all[at, columns(n)], preferred_element_type=jnp.float32)
            if first:
                acc[:, columns(n)] = term
            else:
                total = (acc[:, columns(n)] + term).astype(jnp.bfloat16)
                p_all[own, columns(n)] = total
                acc[:, columns(n)] = -total.astype(jnp.float32)

    all_of(h_all, (nz - 1) * part, h_send, h_sib.at[0]).wait_recv()
    project(yh, True)
    all_of(h_all, nz * part, h_send, h_sib.at[1]).wait_recv()
    project(1 - yh, False)

    to, to_sib, _ = spread(p_all, p_send, p_recv, p_sib, True)
    to(across, x, y, B)
    to(ahead, x, y, A)
    to(behind, x, y, A)
    to_sib(x, y, A)
    to_sib(x, y, B)
    p_one, p_two, p_three, p_four = relays(p_all, p_send, p_recv, p_sib, True)

    m_four()
    all_of(m_all, group // NC, m_send, m_sib).wait_recv()

    @pl.loop(0, group // CHUNK)
    def _(n):
        at = pl.ds(pl.multiple_of(n * CHUNK, CHUNK), CHUNK)
        scores = scale * lax.dot_general(
            p_all[own, :], m_all[at, :], NT, preferred_element_type=jnp.float32
        )
        st[:, at] = scores
        top = jnp.max(scores, axis=0, keepdims=True)
        lse[rank, :, at] = top + jnp.log(jnp.sum(jnp.exp(scores - top), axis=0, keepdims=True))

    for k in range(1, RANKS):
        copy(lse.at[rank], lse.at[rank], st_send, st_recv.at[rank], peer(k)).start()
    to(across, x, y, A)
    to(ahead, x, y, B)
    to(behind, x, y, B)
    p_one()
    for k in range(1, RANKS):
        device = peer(k)
        other = device["rep_0"] * 4 + device["rep_1"] * 2 + device["rep_2"]
        copy(lse.at[other], lse.at[other], st_send, st_recv.at[other], sibling).wait_recv()
    parts = lse[...]
    top = jnp.max(parts, axis=0)
    lt[...] = top + jnp.log(jnp.sum(jnp.exp(parts - top[None]), axis=0))

    @pl.loop(0, group // CHUNK)
    def _(n):
        at = pl.ds(pl.multiple_of(n * CHUNK, CHUNK), CHUNK)
        ct[:, at] = jnp.exp(st[:, at] - lt[:, at]).astype(jnp.bfloat16)

    block = st[:, own]
    diagonal = lax.broadcasted_iota(jnp.int32, block.shape, 0) == lax.broadcasted_iota(
        jnp.int32, block.shape, 1
    )
    own_total = lt[:, own]
    loss_ref[...] = own_total - jnp.sum(jnp.where(diagonal, block, 0.0), axis=0, keepdims=True)
    total_rows = jnp.broadcast_to(own_total, (rows, rows)).T[:, :1]
    p_two()

    @pl.loop(0, width // CHUNK)
    def _(n):
        total = jnp.dot(ct[...], m_all[:, columns(n)], preferred_element_type=jnp.float32)
        total = total - m_all[own, columns(n)].astype(jnp.float32)
        dp[:, columns(n)] = (scale * total).astype(jnp.bfloat16)

    p_three()

    @pl.loop(0, width // CHUNK)
    def _(n):
        grad = lax.dot_general(dp[...], h_all[columns(n), :], NT, preferred_element_type=jnp.float32)
        out_v[1, :, columns(n)] = grad.astype(jnp.bfloat16)

    put_state = pltpu.make_async_copy(out_v.at[1], sg_ref, out_sem.at[0])
    put_state.start()

    def chip(cx, cy):
        for piece in (A, B):
            here = p_all.at[place(cx, cy, co, piece)]
            copy(here, here, p_send, p_sib.at[index(cx, cy, piece)], sibling).wait_recv()
        at = pl.ds(pl.multiple_of((cx * 4 + cy * 2) * rows, NC * rows), NC * rows)
        scores = scale * lax.dot_general(
            m_all[own, :], p_all[at, :], NT, preferred_element_type=jnp.float32
        )
        share = jnp.exp(scores - total_rows).astype(jnp.bfloat16)

        @pl.loop(0, width // CHUNK)
        def _(n):
            acc[:, columns(n)] += jnp.dot(
                share, p_all[at, columns(n)], preferred_element_type=jnp.float32
            )

    chip(x, y)
    chip(x, yo)
    chip(xa, y)
    chip(xb, y)
    p_four()
    chip(x2, y)
    chip(xa, yo)
    chip(xb, yo)
    chip(x2, yo)

    @pl.loop(0, width // CHUNK)
    def _(n):
        out_v[0, :, columns(n)] = (scale * acc[:, columns(n)]).astype(jnp.bfloat16)

    put_mention = pltpu.make_async_copy(out_v.at[0], mg_ref, out_sem.at[1])
    put_mention.start()
    sent = 9 + 5 + 2 * NX * NY
    all_of(m_all, sent * half, m_send, m_sib).wait_send()
    all_of(p_all, sent * half, p_send, m_sib).wait_send()
    pieces = (nz - 1) + nz + (nz - 1) + nz
    all_of(h_all, pieces * part, h_send, m_sib).wait_send()
    view = lse.at[pl.ds(0, RANKS - 1)]
    copy(view, view, st_send, m_sib, sibling).wait_send()
    put_state.wait()
    put_mention.wait()


def local(nz, mentions, entity_states, head):
    rows, width = mentions.shape
    group = rows * RANKS
    bf16, f32 = jnp.bfloat16, jnp.float32
    pieces = 2 * NX * NY
    dma = pltpu.SemaphoreType.DMA
    any_spec = pl.BlockSpec(memory_space=pl.ANY)
    loss, mention_grad, state_grad = pl.pallas_call(
        functools.partial(kernel, nz, 3.0 / math.sqrt(width)),
        out_shape=(
            jax.ShapeDtypeStruct((1, rows), f32),
            jax.ShapeDtypeStruct((rows, width), bf16),
            jax.ShapeDtypeStruct((rows, width), bf16),
        ),
        in_specs=[any_spec] * 3,
        out_specs=(pl.BlockSpec(memory_space=pltpu.VMEM), any_spec, any_spec),
        scratch_shapes=[
            pltpu.VMEM((group, width), bf16),
            pltpu.VMEM((group, width), bf16),
            pltpu.VMEM((width, width), bf16),
            pltpu.VMEM((rows, width), bf16),
            pltpu.VMEM((rows, width), f32),
            pltpu.VMEM((rows, group), f32),
            pltpu.VMEM((rows, group), bf16),
            pltpu.VMEM((RANKS, 1, group), f32),
            pltpu.VMEM((1, group), f32),
            pltpu.VMEM((rows, width), bf16),
            pltpu.VMEM((2, rows, width), bf16),
            dma((3,)),
            dma((pieces,)),
            dma,
            dma((pieces,)),
            dma((pieces,)),
            dma((nz,)),
            dma((nz,)),
            dma((2,)),
            dma((RANKS,)),
            dma, dma, dma, dma,
            dma((2,)),
        ],
        compiler_params=pltpu.CompilerParams(collective_id=0, has_side_effects=True),
    )(mentions, entity_states, head)
    return loss.reshape(rows), mention_grad, state_grad


def solution(mesh):
    torus = Mesh(mesh.devices.reshape(2, 16, 4, 2, 2), DP_REP)
    in_specs = (P(DP_REP, None), P(DP_REP, None), P(("dp_0", "dp_1"), None))
    out_specs = (P(DP_REP), P(DP_REP, None), P(DP_REP, None))
    return jax.shard_map(
        functools.partial(local, 16), mesh=torus, in_specs=in_specs, out_specs=out_specs, check_vma=False
    )
```

time: 162 us -> 79.2 us (0.49)
  Pallas kernels: 0 us -> 74.8 us
  blocking collectives: 49.4 us -> 0 us
  waiting for transfers between devices: 45.6 us -> 0 us
  starting transfers between devices: 20.7 us -> 0 us
  local copies, waits for them, and re-layouts: 17.2 us -> 3.56 us
  matrix products: 13.6 us -> 0 us
  between operations: 14.1 us -> 0.65 us
    pallas_call x0 -> x1, Pallas kernels: none -> 74.8 us  [local(): pl.pallas_call(functools.partial(kernel, nz, 3.0 / math.sqrt(width)), out...]
    all_to_all x2 -> x0, blocking collectives: 41.5 us -> none  [sent_to_all(): lax.all_to_all(jnp.broadcast_to(array[None], (count, *array.shape)), axis...]
    all_gather x1 -> x0, waiting for transfers between devices: 27.4 us -> none  [stacked_from(): blocks = lax.all_gather(blocks, axes[k])]
    all_to_all x3 -> x0, starting transfers between devices: 20.7 us -> none  [sent_to_all(): lax.all_to_all(jnp.broadcast_to(array[None], (count, *array.shape)), axis...]
    all_to_all x3 -> x0, waiting for transfers between devices: 18.3 us -> none  [sent_to_all(): lax.all_to_all(jnp.broadcast_to(array[None], (count, *array.shape)), axis...]
    dot_general x5 -> x0, matrix products: 13.6 us -> none  [the longest x2 5.12 us: score(): lax.dot_general(left_rows, right_rows, contract, preferred_element_type=j...]
    broadcast_in_dim x5 -> x0, local copies, waits for them, and re-layouts: 8.05 us -> none  [sent_to_all(): jnp.broadcast_to(array[None], (count, *array.shape))]
    all_gather x1 -> x0, blocking collectives: 7.94 us -> none  [stacked_from(): blocks = lax.all_gather(blocks, axes[k])]
  transfers between devices with their start and end apart: 4 -> 0, of which waited for: 3 -> 0; matrix products, arithmetic and copies ran while one was open for 9% -> 0% of each run, Pallas kernels for 0% -> 0%
where the time goes in v1:
time: 79.2 us; the launch traced here: 79 us
  Pallas kernels  74.8 us (94%)
  local copies, waits for them, and re-layouts  3.56 us (4%)
    pallas_call x1, Pallas kernels, local(): pl.pallas_call(functools.partial(kernel, nz, 3.0 / math.sqrt(width)), out...  74.8 us
    unnamed x7, local copies, waits for them, and re-layouts  3.56 us

profile of v1, /device:TPU:1, one launch (start us, length us, event | category | flops | bytes accessed | tf_op | source)
XLA Modules:
  0.0 79.0 jit_solution(14192936567562193762)
XLA Ops:
  0.6 74.8 %shard_map.58 = (f32[1,128]{1,0:T(1,128)}, bf16[128,1024]{1,0:T(8,128)(2,1)}, bf16[128,1024]{1,0:T(8,128)(2,1)}) custom-call(bf16[128,1024]{1,0:T(8,128)(2,1)} %m_ref.1, bf16[128,1024]{1,0:T(8,128)(2,1)} %e_ref.1, bf16[32,1024]{1,0:T(8,128)(2,1)} %h_ref.1), custom_call_target="tpu_custom_call" | custom-call | tf_op jit(solution)/shard_map/pallas_call | solution.py:340
  75.5 0.0 copy-start.1
  75.5 0.6 copy-done.1
  76.1 0.5 copy.9
  76.6 0.0 copy-start
  76.6 1.7 %copy.10 = bf16[128,1024]{1,0:T(8,128)(2,1)} copy(bf16[128,1024]{1,0:T(8,128)(2,1)} %get-tuple-element.13) | data formatting | bytes 524288
  78.3 0.0 copy-done
  78.3 0.7 copy.11
Async XLA Ops:
  75.5 0.6 copy-start.1
  76.6 1.7 %copy-start = (bf16[128,1024]{1,0:T(8,128)(2,1)S(1)}, bf16[128,1024]{1,0:T(8,128)(2,1)}, u32[]{:S(2)}) copy-start(bf16[128,1024]{1,0:T(8,128)(2,1)} %get-tuple-element.14) | copy-start | bytes 786436

commit v2 on v1

v2 whole, which is shorter than its diff:
```python
import functools
import math

import jax
import jax.numpy as jnp
from jax import lax
from jax.experimental import pallas as pl
from jax.experimental.pallas import tpu as pltpu
from jax.sharding import Mesh
from jax.sharding import PartitionSpec as P

DP_REP = ("dp_0", "dp_1", "rep_0", "rep_1", "rep_2")
MESH = pl.DeviceIdType.MESH
NX, NY, NC = 4, 2, 2
RANKS = NX * NY * NC
CHUNK = 256
NT = (((1,), (1,)), ((), ()))


def kernel(
    nz, scale,
    m_ref, e_ref, h_ref,
    loss_ref, mg_ref, sg_ref,
    m_all, e_all, p_all, h_all, acc, st, ct, lse, lt, dp,
    local_sem, m_recv, m_sib, e_recv, p_sib, hz_recv, hy_recv, h_sib, st_recv,
    m_send, e_send, p_send, h_send, st_send,
):
    rows, width = m_ref.shape
    half = rows // 2
    shard = h_ref.shape[0]
    part = shard // NC
    group = rows * RANKS
    yh, z = lax.axis_index("dp_0"), lax.axis_index("dp_1")
    x, y, c = lax.axis_index("rep_0"), lax.axis_index("rep_1"), lax.axis_index("rep_2")
    xa, xb, x2 = lax.rem(x + 1 + 2 * c, NX), lax.rem(x + 3 - 2 * c, NX), lax.rem(x + 2, NX)
    yo, co = 1 - y, 1 - c
    rank = x * 4 + y * 2 + c
    ahead, behind, across, sibling = {"rep_0": xa}, {"rep_0": xb}, {"rep_1": yo}, {"rep_2": co}
    partner = {"dp_0": 1 - yh, "rep_1": yo}

    def zat(d):
        return lax.rem(z + nz + d * (1 - 2 * c), nz)

    def along(d):
        return {"dp_1": zat(d)}

    def peer(k):
        return {
            "rep_0": lax.rem(x + k // 4, NX),
            "rep_1": lax.rem(y + (k // 2) % 2, NY),
            "rep_2": lax.rem(c + k % 2, NC),
        }

    barrier = pltpu.get_barrier_semaphore()
    friends = [along(d) for d in (4, -4, 2, -2, 1, -1)] + [partner]
    friends += [peer(k) for k in range(1, RANKS)]
    for device in friends:
        pl.semaphore_signal(barrier, inc=1, device_id=device, device_id_type=MESH)
    own = pl.ds(pl.multiple_of(rank * rows, rows), rows)
    own_chip = pl.ds(pl.multiple_of((x * NY + y) * rows, rows), rows)
    own_shard = pl.ds(pl.multiple_of((yh * nz + z) * shard, shard), shard)
    fills = [
        pltpu.make_async_copy(m_ref, m_all.at[own], local_sem.at[0]),
        pltpu.make_async_copy(e_ref, e_all.at[own_chip], local_sem.at[1]),
        pltpu.make_async_copy(h_ref, h_all.at[own_shard], local_sem.at[2]),
    ]
    for fill in fills:
        fill.start()
    pl.semaphore_wait(barrier, len(friends))

    def copy(src, dst, send_sem, recv_sem, device):
        return pltpu.make_async_remote_copy(
            src_ref=src, dst_ref=dst, send_sem=send_sem, recv_sem=recv_sem,
            device_id=device, device_id_type=MESH,
        )

    A, B = 0, 1

    def index(cx, cy, piece):
        return piece * (NX * NY) + cx * NY + cy

    def m_place(cx, cy, piece):
        return m_all.at[pl.ds(pl.multiple_of((cx * 4 + cy * 2 + c) * rows + piece * half, half), half)]

    def e_place(cx, cy, piece):
        return e_all.at[pl.ds(pl.multiple_of((cx * NY + cy) * rows + piece * half, half), half)]

    def m_to(device, cx, cy, piece, src=None):
        here = m_place(cx, cy, piece)
        recv = m_recv.at[index(cx, cy, piece)]
        copy(here if src is None else src, here, m_send, recv, device).start()

    def m_over(cx, cy, piece, src=None):
        here = m_place(cx, cy, piece)
        copy(here if src is None else src, here, m_send, m_sib, sibling).start()

    def m_step(cx, cy, piece, *devices):
        here = m_place(cx, cy, piece)
        copy(here, here, m_send, m_recv.at[index(cx, cy, piece)], sibling).wait_recv()
        for device in devices:
            m_to(device, cx, cy, piece)
        m_over(cx, cy, piece)

    def e_to(device, cx, cy, piece, src=None):
        here = e_place(cx, cy, piece)
        recv = e_recv.at[index(cx, cy, piece)]
        copy(here if src is None else src, here, e_send, recv, device).start()

    def e_step(cx, cy, piece, *devices):
        here = e_place(cx, cy, piece)
        copy(here, here, e_send, e_recv.at[index(cx, cy, piece)], sibling).wait_recv()
        for device in devices:
            e_to(device, cx, cy, piece)

    def one(step):
        step(xb, y, A, ahead, across)
        step(x, yo, B, ahead, behind)
        step(xa, y, A, across)

    def two(step):
        step(x, yo, A)
        step(xa, y, B, behind)
        step(xb, y, B)

    def h_place(cy, cz):
        return h_all.at[pl.ds(pl.multiple_of((cy * nz + cz) * shard + c * part, part), part)]

    def h_to(device, recv, cy, cz, src=None):
        here = h_place(cy, cz)
        copy(here if src is None else src, here, h_send, recv, device).start()

    def h_got(recv, cy, cz):
        here = h_place(cy, cz)
        copy(here, here, h_send, recv, sibling).wait_recv()

    def h_step(d, *steps):
        cz = zat(d)
        h_got(hz_recv.at[cz], yh, cz)
        for step in steps:
            h_to(along(step), hz_recv.at[cz], yh, cz)
        h_to(partner, hy_recv.at[cz], yh, cz)
        h_to(sibling, h_sib.at[0], yh, cz)

    def crossed(*ds):
        for d in ds:
            cz = zat(d)
            h_got(hy_recv.at[cz], 1 - yh, cz)
            h_to(sibling, h_sib.at[1], 1 - yh, cz)

    h_own = h_ref.at[pl.ds(pl.multiple_of(c * part, part), part)]
    for d in (4, -4, 2, 1, -1):
        h_to(along(d), hz_recv.at[z], yh, z, h_own)
    h_to(partner, hy_recv.at[z], yh, z, h_own)
    m_half = [m_ref.at[pl.ds(piece * half, half)] for piece in (A, B)]
    e_half = [e_ref.at[pl.ds(piece * half, half)] for piece in (A, B)]
    m_to(across, x, y, B, m_half[B])
    m_to(ahead, x, y, A, m_half[A])
    m_to(behind, x, y, A, m_half[A])
    m_to(across, x, y, A, m_half[A])
    m_to(ahead, x, y, B, m_half[B])
    m_to(behind, x, y, B, m_half[B])
    e_to(across, x, y, B, e_half[B])
    m_over(x, y, A, m_half[A])
    m_over(x, y, B, m_half[B])

    h_step(-1)
    h_step(1)
    h_step(-2)
    h_step(-4, 4, 2, 1, -1)
    h_step(4, 2, 1, -1)
    one(m_step)
    e_to(ahead, x, y, A, e_half[A])
    e_to(behind, x, y, A, e_half[A])
    e_to(across, x, y, A, e_half[A])
    e_to(ahead, x, y, B, e_half[B])
    e_to(behind, x, y, B, e_half[B])
    crossed(0)
    for d in (-5, 3, -3, 5, -6, 2):
        h_step(d)
    crossed(-1, 1, -2)
    h_step(8, 2, 1, -1)
    two(m_step)
    crossed(-4, 4)
    m_step(x2, y, A, across)
    m_step(xb, yo, B, ahead)
    m_step(xb, yo, A)
    m_step(xa, yo, A)
    m_step(xa, yo, B)
    one(e_step)
    for d in (7, -7, 6):
        h_step(d)
    crossed(-5, 3, -3, 5, -6, 2, 8)
    two(e_step)
    m_step(x2, y, B)
    m_step(x2, yo, A)
    m_step(x2, yo, B)
    crossed(7, -7, 6)
    for fill in fills:
        fill.wait()

    def all_of(ref, count, send_sem, recv_sem):
        view = ref.at[pl.ds(0, count)]
        return copy(view, view, send_sem, recv_sem, sibling)

    def columns(n):
        return pl.ds(pl.multiple_of(n * CHUNK, CHUNK), CHUNK)

    all_of(h_all, (nz - 1) * part, h_send, h_sib.at[0]).wait_recv()
    all_of(h_all, nz * part, h_send, h_sib.at[1]).wait_recv()

    def p_place(cx, cy, core):
        return p_all.at[pl.ds(pl.multiple_of((cx * 4 + cy * 2 + core) * rows, rows), rows)]

    def project(cx, cy):
        at = pl.ds(pl.multiple_of((cx * NY + cy) * rows, rows), rows)
        to = pl.ds(pl.multiple_of((cx * 4 + cy * 2 + c) * rows, rows), rows)

        @pl.loop(0, width // CHUNK)
        def _(n):
            p_all[to, columns(n)] = jnp.dot(
                e_all[at, :], h_all[:, columns(n)], preferred_element_type=jnp.float32
            ).astype(jnp.bfloat16)

        here = p_place(cx, cy, c)
        copy(here, here, p_send, p_sib.at[cx * NY + cy], sibling).start()

    project(x, y)
    all_of(m_all, group // NC, m_send, m_sib).wait_recv()

    @pl.loop(0, group // CHUNK)
    def _(n):
        at = columns(n)
        scores = scale * lax.dot_general(
            p_all[own, :], m_all[at, :], NT, preferred_element_type=jnp.float32
        )
        st[:, at] = scores
        top = jnp.max(scores, axis=0, keepdims=True)
        lse[rank, :, at] = top + jnp.log(jnp.sum(jnp.exp(scores - top), axis=0, keepdims=True))

    for k in range(1, RANKS):
        copy(lse.at[rank], lse.at[rank], st_send, st_recv.at[rank], peer(k)).start()
    project(x, yo)
    e_step(x2, y, A)
    e_step(xb, yo, B, ahead)
    e_step(xb, yo, A, ahead)
    project(xa, y)
    project(xb, y)
    for k in range(1, RANKS):
        device = peer(k)
        other = device["rep_0"] * 4 + device["rep_1"] * 2 + device["rep_2"]
        copy(lse.at[other], lse.at[other], st_send, st_recv.at[other], sibling).wait_recv()
    parts = lse[...]
    top = jnp.max(parts, axis=0)
    lt[...] = top + jnp.log(jnp.sum(jnp.exp(parts - top[None]), axis=0))

    @pl.loop(0, group // CHUNK)
    def _(n):
        at = columns(n)
        ct[:, at] = jnp.exp(st[:, at] - lt[:, at]).astype(jnp.bfloat16)

    block = st[:, own]
    diagonal = lax.broadcasted_iota(jnp.int32, block.shape, 0) == lax.broadcasted_iota(
        jnp.int32, block.shape, 1
    )
    own_total = lt[:, own]
    loss_ref[...] = own_total - jnp.sum(jnp.where(diagonal, block, 0.0), axis=0, keepdims=True)
    total_rows = jnp.broadcast_to(own_total, (rows, rows)).T[:, :1]

    @pl.loop(0, width // CHUNK)
    def _(n):
        total = jnp.dot(ct[...], m_all[:, columns(n)], preferred_element_type=jnp.float32)
        total = total - m_all[own, columns(n)].astype(jnp.float32)
        dp[:, columns(n)] = (scale * total).astype(jnp.bfloat16)

    e_step(xa, yo, A)
    e_step(xa, yo, B)

    @pl.loop(0, width // CHUNK)
    def _(n):
        grad = lax.dot_general(dp[...], h_all[columns(n), :], NT, preferred_element_type=jnp.float32)
        sg_ref[:, columns(n)] = grad.astype(jnp.bfloat16)
        acc[:, columns(n)] = -p_all[own, columns(n)].astype(jnp.float32)

    def chip(cx, cy):
        here = p_place(cx, cy, co)
        copy(here, here, p_send, p_sib.at[cx * NY + cy], sibling).wait_recv()
        at = pl.ds(pl.multiple_of((cx * 4 + cy * 2) * rows, NC * rows), NC * rows)
        scores = scale * lax.dot_general(
            m_all[own, :], p_all[at, :], NT, preferred_element_type=jnp.float32
        )
        share = jnp.exp(scores - total_rows).astype(jnp.bfloat16)

        @pl.loop(0, width // CHUNK)
        def _(n):
            acc[:, columns(n)] += jnp.dot(
                share, p_all[at, columns(n)], preferred_element_type=jnp.float32
            )

    project(xb, yo)
    chip(x, y)
    project(xa, yo)
    chip(x, yo)
    e_step(x2, y, B)
    project(x2, y)
    chip(xa, y)
    chip(xb, y)
    e_step(x2, yo, A)
    e_step(x2, yo, B)
    project(x2, yo)
    chip(xb, yo)
    chip(xa, yo)
    chip(x2, y)
    chip(x2, yo)

    @pl.loop(0, width // CHUNK)
    def _(n):
        mg_ref[:, columns(n)] = (scale * acc[:, columns(n)]).astype(jnp.bfloat16)

    sent = 6 + 5 + 1 + 2
    all_of(m_all, (sent + 2 * NX * NY) * half, m_send, m_sib).wait_send()
    all_of(e_all, sent * half, e_send, m_sib).wait_send()
    all_of(p_all, NX * NY * rows, p_send, m_sib).wait_send()
    pieces = (6 + 6 + 5 + 5 + 12 * 2) + nz
    all_of(h_all, pieces * part, h_send, m_sib).wait_send()
    view = lse.at[pl.ds(0, RANKS - 1)]
    copy(view, view, st_send, m_sib, sibling).wait_send()


def local(nz, mentions, entity_states, head):
    rows, width = mentions.shape
    group = rows * RANKS
    bf16, f32 = jnp.bfloat16, jnp.float32
    pieces = 2 * NX * NY
    dma = pltpu.SemaphoreType.DMA
    any_spec = pl.BlockSpec(memory_space=pl.ANY)
    vmem_spec = pl.BlockSpec(memory_space=pltpu.VMEM)
    loss, mention_grad, state_grad = pl.pallas_call(
        functools.partial(kernel, nz, 3.0 / math.sqrt(width)),
        out_shape=(
            pltpu.VMEM((1, rows), f32),
            pltpu.VMEM((rows, width), bf16),
            pltpu.VMEM((rows, width), bf16),
        ),
        in_specs=[any_spec] * 3,
        out_specs=(vmem_spec,) * 3,
        scratch_shapes=[
            pltpu.VMEM((group, width), bf16),
            pltpu.VMEM((group // NC, width), bf16),
            pltpu.VMEM((group, width), bf16),
            pltpu.VMEM((width, width), bf16),
            pltpu.VMEM((rows, width), f32),
            pltpu.VMEM((rows, group), f32),
            pltpu.VMEM((rows, group), bf16),
            pltpu.VMEM((RANKS, 1, group), f32),
            pltpu.VMEM((1, group), f32),
            pltpu.VMEM((rows, width), bf16),
            dma((3,)),
            dma((pieces,)),
            dma,
            dma((pieces,)),
            dma((NX * NY,)),
            dma((nz,)),
            dma((nz,)),
            dma((2,)),
            dma((RANKS,)),
            dma, dma, dma, dma, dma,
        ],
        compiler_params=pltpu.CompilerParams(collective_id=0, has_side_effects=True),
    )(mentions, entity_states, head)
    return loss.reshape(rows), mention_grad, state_grad


def solution(mesh):
    torus = Mesh(mesh.devices.reshape(2, 16, 4, 2, 2), DP_REP)
    in_specs = (P(DP_REP, None), P(DP_REP, None), P(("dp_0", "dp_1"), None))
    out_specs = (P(DP_REP), P(DP_REP, None), P(DP_REP, None))
    return jax.shard_map(
        functools.partial(local, 16), mesh=torus, in_specs=in_specs, out_specs=out_specs, check_vma=False
    )
```

time: 79.2 us -> 65.2 us (0.82)
  Pallas kernels: 74.8 us -> 62.5 us
  local copies, waits for them, and re-layouts: 3.56 us -> 1.92 us
    pallas_call x1, Pallas kernels: 74.8 us -> 62.5 us  [local(): pl.pallas_call(functools.partial(kernel, nz, 3.0 / math.sqrt(width)), out...]
    unnamed x7 -> x3, local copies, waits for them, and re-layouts: 3.56 us -> 1.92 us
where the time goes in v2:
time: 65.2 us; the launch traced here: 65.1 us
  Pallas kernels  62.5 us (96%)
  local copies, waits for them, and re-layouts  1.92 us (3%)
    pallas_call x1, Pallas kernels, local(): pl.pallas_call(functools.partial(kernel, nz, 3.0 / math.sqrt(width)), out...  62.5 us
    unnamed x3, local copies, waits for them, and re-layouts  1.92 us

profile of v2, /device:TPU:1, one launch (start us, length us, event | category | flops | bytes accessed | tf_op | source)
XLA Modules:
  0.0 65.1 jit_solution(10767773823799139931)
XLA Ops:
  0.6 62.5 %shard_map.58 = (f32[1,128]{1,0:T(1,128)S(1)}, bf16[128,1024]{1,0:T(8,128)(2,1)S(1)}, bf16[128,1024]{1,0:T(8,128)(2,1)S(1)}) custom-call(bf16[128,1024]{1,0:T(8,128)(2,1)} %m_ref.1, bf16[128,1024]{1,0:T(8,128)(2,1)} %e_ref.1, bf16[32,1024]{1,0:T(8,128)(2,1)} %h_ref.1), custom_call_target="tpu_custom_call" | custom-call | tf_op jit(solution)/shard_map/pallas_call | solution.py:337
  63.1 0.5 copy.9
  63.7 0.7 %copy.10 = bf16[128,1024]{1,0:T(8,128)(2,1)} copy(bf16[128,1024]{1,0:T(8,128)(2,1)S(1)} %get-tuple-element.10) | data formatting | bytes 524288
  64.4 0.7 %copy.11 = bf16[128,1024]{1,0:T(8,128)(2,1)} copy(bf16[128,1024]{1,0:T(8,128)(2,1)S(1)} %get-tuple-element.11) | data formatting | bytes 524288

commit v3 on v2

v3 whole, which is shorter than its diff:
```python
import functools
import math

import jax
import jax.numpy as jnp
from jax import lax
from jax.experimental import pallas as pl
from jax.experimental.pallas import tpu as pltpu
from jax.sharding import Mesh
from jax.sharding import PartitionSpec as P

DP_REP = ("dp_0", "dp_1", "rep_0", "rep_1", "rep_2")
MESH = pl.DeviceIdType.MESH
NX, NY, NC = 4, 2, 2
RANKS = NX * NY * NC
CHUNK = 256
WIDE = 512
BITS = 2
NT = (((1,), (1,)), ((), ()))


def kernel(
    nz, scale,
    m_ref, e_ref, h_ref,
    loss_ref, mg_ref, sg_ref,
    m_all, e_all, p_all, h_all, st, ct, lse, lt, dp,
    local_sem, m_recv, m_sib, e_recv, e_sib, p_sib, hz_recv, hy_recv, h_sib, st_recv,
    m_send, e_send, p_send, h_send, st_send, ready,
):
    rows, width = m_ref.shape
    shard = h_ref.shape[0]
    bit = rows // BITS
    group = rows * RANKS
    yh, z = lax.axis_index("dp_0"), lax.axis_index("dp_1")
    x, y, c = lax.axis_index("rep_0"), lax.axis_index("rep_1"), lax.axis_index("rep_2")
    xa, xb, x2 = lax.rem(x + 1, NX), lax.rem(x + 3, NX), lax.rem(x + 2, NX)
    yo, co = 1 - y, 1 - c
    rank = x * 4 + y * 2 + c
    across, sibling = {"rep_1": yo}, {"rep_2": co}
    plus, minus = {"rep_0": xa}, {"rep_0": xb}
    head, bulk = c == 0, c == 1

    def zat(d):
        return lax.rem(z + nz + d, nz)

    def along(d):
        return {"dp_1": zat(d)}

    def beyond(d):
        return {"dp_0": 1 - yh, "rep_1": yo, "dp_1": zat(d)}

    def peer(k):
        return {
            "rep_0": lax.rem(x + k // 4, NX),
            "rep_1": lax.rem(y + (k // 2) % 2, NY),
            "rep_2": lax.rem(c + k % 2, NC),
        }

    def signal(sem, device):
        pl.semaphore_signal(sem, inc=1, device_id=device, device_id_type=MESH)

    barrier = pltpu.get_barrier_semaphore()
    for k in range(1, RANKS):
        signal(barrier, peer(k))

    @pl.when(head)
    def _():
        for device in [along(-3), along(-2), along(-1), beyond(0), beyond(-1), beyond(-2)]:
            signal(barrier, device)

    own = pl.ds(pl.multiple_of(rank * rows, rows), rows)
    own_shard = pl.ds(pl.multiple_of((yh * nz + z) * shard, shard), shard)
    fills = [
        pltpu.make_async_copy(m_ref, m_all.at[own], local_sem.at[0]),
        pltpu.make_async_copy(e_ref, e_all.at[own], local_sem.at[1]),
        pltpu.make_async_copy(h_ref, h_all.at[own_shard], local_sem.at[2]),
    ]
    for fill in fills:
        fill.start()

    def copy(src, dst, send_sem, recv_sem, device):
        return pltpu.make_async_remote_copy(
            src_ref=src, dst_ref=dst, send_sem=send_sem, recv_sem=recv_sem,
            device_id=device, device_id_type=MESH,
        )

    A, B = 0, 1

    def chip(cx, cy):
        return cx * NY + cy

    def index(cx, cy, piece):
        return piece * (NX * NY) + chip(cx, cy)

    def place(array, cx, cy, piece):
        return array.at[pl.ds(pl.multiple_of((cx * 4 + cy * 2 + piece) * rows, rows), rows)]

    def bulk_of(array, send_sem, recv, over, ahead, behind, xa, xb):
        def here(cx, cy, piece, k):
            return place(array, cx, cy, piece).at[pl.ds(k * bit, bit)]

        def to(device, cx, cy, piece, k, src=None):
            at = here(cx, cy, piece, k)
            recv_sem = recv.at[index(cx, cy, piece) * BITS + k]
            copy(at if src is None else src.at[pl.ds(k * bit, bit)], at, send_sem, recv_sem, device).start()

        def got(cx, cy, piece, k):
            at = here(cx, cy, piece, k)
            copy(at, at, send_sem, recv.at[index(cx, cy, piece) * BITS + k], sibling).wait_recv()

        def step(cx, cy, piece, *devices):
            for k in range(BITS):
                got(cx, cy, piece, k)
                for device in devices:
                    to(device, cx, cy, piece, k)
                over(here(cx, cy, piece, k), cx, cy, piece)

        def start(source):
            for k in range(BITS):
                for device in (across, ahead, behind):
                    to(device, x, y, B, k, source)
            for k in range(BITS):
                got(x, y, A, k)
                for device in (ahead, behind, across):
                    to(device, x, y, A, k)

        def one():
            step(x, yo, B, ahead, behind)
            step(xa, y, B, behind)
            step(xb, y, B)
            step(xb, y, A, ahead, across)

        def two():
            step(xa, y, A, across)
            step(x, yo, A)
            step(xb, yo, B, ahead)
            step(xa, yo, B)

        def three():
            step(x2, y, B)
            step(x2, y, A, across)
            step(xb, yo, A)
            step(xa, yo, A)

        def four():
            step(x2, yo, B)
            step(x2, yo, A)

        return start, one, two, three, four

    def m_over(here, cx, cy, piece):
        copy(here, here, m_send, m_sib, sibling).start()

    def e_over(here, cx, cy, piece):
        if piece == A:
            copy(here, here, e_send, e_sib.at[chip(cx, cy)], sibling).start()

    def wait_sent(ref, sem, total):
        most = ref.shape[0]
        while total > 0:
            view = ref.at[pl.ds(0, min(total, most))]
            copy(view, view, sem, m_sib, sibling).wait_send()
            total -= most

    def wait_got(ref, sem, total):
        view = ref.at[pl.ds(0, total)]
        copy(view, view, m_send, sem, sibling).wait_recv()

    @pl.when(bulk)
    def _():
        pl.semaphore_wait(barrier, RANKS - 1)
        m_start, m_one, m_two, m_three, m_four = bulk_of(
            m_all, m_send, m_recv, m_over, plus, minus, xa, xb
        )
        e_start, e_one, e_two, e_three, e_four = bulk_of(
            e_all, e_send, e_recv, e_over, minus, plus, xb, xa
        )
        m_start(m_ref)
        copy(m_ref, place(m_all, x, y, B), m_send, m_sib, sibling).start()
        m_one()
        e_start(e_ref)
        m_two()
        m_three()
        e_one()
        m_four()
        e_two()
        e_three()
        e_four()

    def h_place(cy, cz):
        return h_all.at[pl.ds(pl.multiple_of((cy * nz + cz) * shard, shard), shard)]

    def h_to(device, recv, cy, cz, src=None):
        here = h_place(cy, cz)
        copy(here if src is None else src, here, h_send, recv.at[cz] if device is not sibling else recv, device).start()

    def h_got(recv, cy, d):
        here = h_place(cy, zat(d))
        copy(here, here, h_send, recv.at[zat(d)], sibling).wait_recv()

    def h_line(d, jumps, near):
        h_got(hz_recv, yh, d)
        cz = zat(d)
        for step in jumps:
            h_to(along(step), hz_recv, yh, cz)
        for step in near:
            h_to(along(step), hz_recv, yh, cz)
            h_to(beyond(step), hy_recv, yh, cz)
        h_to(beyond(0), hy_recv, yh, cz)
        h_to(sibling, h_sib, yh, cz)

    def h_leaf(*ds):
        for d in ds:
            h_got(hz_recv, yh, d)
            h_to(sibling, h_sib, yh, zat(d))

    def crossed(*ds):
        for d in ds:
            h_got(hy_recv, 1 - yh, d)
            h_to(sibling, h_sib, 1 - yh, zat(d))

    def give(source, array, send_sem, recv):
        for k in range(BITS):
            at = pl.ds(k * bit, bit)
            recv_sem = recv.at[index(x, y, A) * BITS + k]
            copy(source.at[at], place(array, x, y, A).at[at], send_sem, recv_sem, sibling).start()

    @pl.when(head)
    def _():
        pl.semaphore_wait(barrier, RANKS + 5)
        for device in [along(3), along(1), beyond(1)]:
            signal(ready, device)
        give(m_ref, m_all, m_send, m_recv)
        h_to(along(3), hz_recv, yh, z, h_ref)
        h_to(along(1), hz_recv, yh, z, h_ref)
        h_to(beyond(1), hy_recv, yh, z, h_ref)
        h_to(beyond(0), hy_recv, yh, z, h_ref)
        give(e_ref, e_all, e_send, e_recv)
        pl.semaphore_wait(ready, 3)
        h_to(along(-3), hz_recv, yh, z, h_ref)
        h_to(along(-1), hz_recv, yh, z, h_ref)
        h_to(beyond(-1), hy_recv, yh, z, h_ref)
        h_leaf(-1)
        h_line(-3, (3,), (1, -1))
        h_leaf(1)
        h_line(3, (-3,), (1, -1))
        crossed(0, -1, 1)
        h_leaf(-4, 2, 4, -2)
        h_line(-6, (), (2, 1, -1))
        crossed(-3, 3)
        h_line(6, (), (1, -1))
        crossed(-4, 2, 4, -2)
        h_leaf(-7, 5, 7, -5, 8)
        crossed(-6, 6, -7, 5, 7, -5, 8)

    for fill in fills:
        fill.wait()

    @pl.when(bulk)
    def _():
        wait_got(h_all, h_sib, (2 * nz - 1) * shard)

    def columns(n, size=CHUNK):
        return pl.ds(pl.multiple_of(n * size, size), size)

    def project(*chips):
        at = [pl.ds(pl.multiple_of((cx * 4 + cy * 2 + c) * rows, rows), rows) for cx, cy in chips]

        @pl.loop(0, width // CHUNK)
        def _(n):
            for block in at:
                p_all[block, columns(n)] = jnp.dot(
                    e_all[block, :], h_all[:, columns(n)], preferred_element_type=jnp.float32
                ).astype(jnp.bfloat16)

        for cx, cy in chips:
            here = place(p_all, cx, cy, c)
            copy(here, here, p_send, p_sib.at[chip(cx, cy)], sibling).start()

    project((x, y))

    @pl.when(head)
    def _():
        wait_got(m_all, m_sib, (RANKS - 1) * rows)

    @pl.loop(0, group // WIDE)
    def _(n):
        at = columns(n, WIDE)
        scores = scale * lax.dot_general(
            m_all[at, :], p_all[own, :], NT, preferred_element_type=jnp.float32
        ).T
        st[:, at] = scores
        top = jnp.max(scores, axis=0, keepdims=True)
        lse[rank, :, at] = top + jnp.log(jnp.sum(jnp.exp(scores - top), axis=0, keepdims=True))

    for k in range(1, RANKS):
        copy(lse.at[rank], lse.at[rank], st_send, st_recv.at[rank], peer(k)).start()

    others = [(x, yo), (xa, y), (xb, y), (x2, y), (xa, yo), (xb, yo), (x2, yo)]

    @pl.when(head)
    def _():
        for cx, cy in others:
            here = place(e_all, cx, cy, A)
            copy(here, here, e_send, e_sib.at[chip(cx, cy)], sibling).wait_recv()

    project(*others)
    for k in range(1, RANKS):
        device = peer(k)
        other = device["rep_0"] * 4 + device["rep_1"] * 2 + device["rep_2"]
        copy(lse.at[other], lse.at[other], st_send, st_recv.at[other], sibling).wait_recv()
    parts = lse[...]
    top = jnp.max(parts, axis=0)
    lt[...] = top + jnp.log(jnp.sum(jnp.exp(parts - top[None]), axis=0))

    @pl.loop(0, group // CHUNK)
    def _(n):
        at = columns(n)
        ct[:, at] = jnp.exp(st[:, at] - lt[:, at]).astype(jnp.bfloat16)

    block = st[:, own]
    diagonal = lax.broadcasted_iota(jnp.int32, block.shape, 0) == lax.broadcasted_iota(
        jnp.int32, block.shape, 1
    )
    own_total = lt[:, own]
    loss_ref[...] = own_total - jnp.sum(jnp.where(diagonal, block, 0.0), axis=0, keepdims=True)
    total_rows = jnp.broadcast_to(own_total, (rows, rows)).T[:, :1]

    @pl.loop(0, width // CHUNK)
    def _(n):
        total = jnp.dot(ct[...], m_all[:, columns(n)], preferred_element_type=jnp.float32)
        total = total - m_all[own, columns(n)].astype(jnp.float32)
        dp[:, columns(n)] = (scale * total).astype(jnp.bfloat16)

    @pl.loop(0, width // WIDE)
    def _(n):
        at = columns(n, WIDE)
        grad = lax.dot_general(h_all[at, :], dp[...], NT, preferred_element_type=jnp.float32)
        sg_ref[:, at] = grad.T.astype(jnp.bfloat16)

    for cx, cy in [(x, y)] + others:
        here = place(p_all, cx, cy, co)
        copy(here, here, p_send, p_sib.at[chip(cx, cy)], sibling).wait_recv()

    @pl.loop(0, group // WIDE)
    def _(n):
        at = columns(n, WIDE)
        scores = scale * lax.dot_general(
            p_all[at, :], m_all[own, :], NT, preferred_element_type=jnp.float32
        ).T
        ct[:, at] = jnp.exp(scores - total_rows).astype(jnp.bfloat16)

    @pl.loop(0, width // CHUNK)
    def _(n):
        total = jnp.dot(ct[...], p_all[:, columns(n)], preferred_element_type=jnp.float32)
        total = total - p_all[own, columns(n)].astype(jnp.float32)
        mg_ref[:, columns(n)] = (scale * total).astype(jnp.bfloat16)

    moves = 6 + 4 + 2 + 1 + 1

    @pl.when(bulk)
    def _():
        wait_sent(m_all, m_send, (moves + RANKS - 1) * rows)
        wait_sent(e_all, e_send, (moves + NX * NY - 1) * rows)

    @pl.when(head)
    def _():
        wait_sent(m_all, m_send, rows)
        wait_sent(e_all, e_send, rows)
        wait_sent(h_all, h_send, (7 + 7 + 7 + 8 + 6 + 11 + nz) * shard)

    wait_sent(p_all, p_send, NX * NY * rows)
    view = lse.at[pl.ds(0, RANKS - 1)]
    copy(view, view, st_send, m_sib, sibling).wait_send()


def local(nz, mentions, entity_states, head):
    rows, width = mentions.shape
    group = rows * RANKS
    bf16, f32 = jnp.bfloat16, jnp.float32
    pieces = 2 * NX * NY
    dma = pltpu.SemaphoreType.DMA
    any_spec = pl.BlockSpec(memory_space=pl.ANY)
    vmem_spec = pl.BlockSpec(memory_space=pltpu.VMEM)
    loss, mention_grad, state_grad = pl.pallas_call(
        functools.partial(kernel, nz, 3.0 / math.sqrt(width)),
        out_shape=(
            pltpu.VMEM((1, rows), f32),
            pltpu.VMEM((rows, width), bf16),
            pltpu.VMEM((rows, width), bf16),
        ),
        in_specs=[any_spec] * 3,
        out_specs=(vmem_spec,) * 3,
        scratch_shapes=[
            pltpu.VMEM((group, width), bf16),
            pltpu.VMEM((group, width), bf16),
            pltpu.VMEM((group, width), bf16),
            pltpu.VMEM((width, width), bf16),
            pltpu.VMEM((rows, group), f32),
            pltpu.VMEM((rows, group), bf16),
            pltpu.VMEM((RANKS, 1, group), f32),
            pltpu.VMEM((1, group), f32),
            pltpu.VMEM((rows, width), bf16),
            dma((3,)),
            dma((pieces * BITS,)),
            dma,
            dma((pieces * BITS,)),
            dma((NX * NY,)),
            dma((NX * NY,)),
            dma((nz,)),
            dma((nz,)),
            dma,
            dma((RANKS,)),
            dma, dma, dma, dma, dma,
            pltpu.SemaphoreType.REGULAR,
        ],
        compiler_params=pltpu.CompilerParams(collective_id=0, has_side_effects=True),
    )(mentions, entity_states, head)
    return loss.reshape(rows), mention_grad, state_grad


def solution(mesh):
    torus = Mesh(mesh.devices.reshape(2, 16, 4, 2, 2), DP_REP)
    in_specs = (P(DP_REP, None), P(DP_REP, None), P(("dp_0", "dp_1"), None))
    out_specs = (P(DP_REP), P(DP_REP, None), P(DP_REP, None))
    return jax.shard_map(
        functools.partial(local, 16), mesh=torus, in_specs=in_specs, out_specs=out_specs, check_vma=False
    )
```

time: 65.2 us -> 58.2 us (0.89)
  Pallas kernels: 62.5 us -> 55.5 us
    pallas_call x1, Pallas kernels: 62.5 us -> 55.5 us  [local(): pl.pallas_call(functools.partial(kernel, nz, 3.0 / math.sqrt(width)), out...]
where the time goes in v3:
time: 58.2 us; the launch traced here: 58.1 us
  Pallas kernels  55.5 us (95%)
  local copies, waits for them, and re-layouts  1.92 us (3%)
  between operations  0.64 us (1%)
    pallas_call x1, Pallas kernels, local(): pl.pallas_call(functools.partial(kernel, nz, 3.0 / math.sqrt(width)), out...  55.5 us
    unnamed x3, local copies, waits for them, and re-layouts  1.92 us

profile of v3, /device:TPU:1, one launch (start us, length us, event | category | flops | bytes accessed | tf_op | source)
XLA Modules:
  0.0 58.1 jit_solution(12708594589035580638)
XLA Ops:
  0.6 55.5 %shard_map.58 = (f32[1,128]{1,0:T(1,128)S(1)}, bf16[128,1024]{1,0:T(8,128)(2,1)S(1)}, bf16[128,1024]{1,0:T(8,128)(2,1)S(1)}) custom-call(bf16[128,1024]{1,0:T(8,128)(2,1)} %m_ref.1, bf16[128,1024]{1,0:T(8,128)(2,1)} %e_ref.1, bf16[32,1024]{1,0:T(8,128)(2,1)} %h_ref.1), custom_call_target="tpu_custom_call" | custom-call | tf_op jit(solution)/shard_map/pallas_call | solution.py:385
  56.1 0.5 copy.9
  56.7 0.7 %copy.10 = bf16[128,1024]{1,0:T(8,128)(2,1)} copy(bf16[128,1024]{1,0:T(8,128)(2,1)S(1)} %get-tuple-element.10) | data formatting | bytes 524288
  57.4 0.7 %copy.11 = bf16[128,1024]{1,0:T(8,128)(2,1)} copy(bf16[128,1024]{1,0:T(8,128)(2,1)S(1)} %get-tuple-element.11) | data formatting | bytes 524288

commit v4 on v3

--- a/solution.py
+++ b/solution.py
@@ -95,7 +95,7 @@
     def place(array, cx, cy, piece):
         return array.at[pl.ds(pl.multiple_of((cx * 4 + cy * 2 + piece) * rows, rows), rows)]
 
-    def bulk_of(array, send_sem, recv, over, ahead, behind, xa, xb):
+    def bulk_of(array, send_sem, recv, over, ahead, behind, xa, xb, turn):
         def here(cx, cy, piece, k):
             return place(array, cx, cy, piece).at[pl.ds(k * bit, bit)]
 
@@ -115,9 +115,13 @@
                     to(device, cx, cy, piece, k)
                 over(here(cx, cy, piece, k), cx, cy, piece)
 
+        def first(source):
+            for k in range(BITS):
+                to(across, x, y, B, k, source)
+
         def start(source):
             for k in range(BITS):
-                for device in (across, ahead, behind):
+                for device in (ahead, behind):
                     to(device, x, y, B, k, source)
             for k in range(BITS):
                 got(x, y, A, k)
@@ -138,15 +142,15 @@
 
         def three():
             step(x2, y, B)
-            step(x2, y, A, across)
-            step(xb, yo, A)
+            step(x2, y, A, *(() if turn else (across,)))
+            step(xb, yo, A, *((ahead,) if turn else ()))
             step(xa, yo, A)
 
         def four():
             step(x2, yo, B)
             step(x2, yo, A)
 
-        return start, one, two, three, four
+        return first, start, one, two, three, four
 
     def m_over(here, cx, cy, piece):
         copy(here, here, m_send, m_sib, sibling).start()
@@ -166,25 +170,28 @@
         view = ref.at[pl.ds(0, total)]
         copy(view, view, m_send, sem, sibling).wait_recv()
 
+    m_first, m_start, m_one, m_two, m_three, m_four = bulk_of(
+        m_all, m_send, m_recv, m_over, plus, minus, xa, xb, False
+    )
+    e_first, e_start, e_one, e_two, e_three, e_four = bulk_of(
+        e_all, e_send, e_recv, e_over, minus, plus, xb, xa, True
+    )
+
     @pl.when(bulk)
     def _():
         pl.semaphore_wait(barrier, RANKS - 1)
-        m_start, m_one, m_two, m_three, m_four = bulk_of(
-            m_all, m_send, m_recv, m_over, plus, minus, xa, xb
-        )
-        e_start, e_one, e_two, e_three, e_four = bulk_of(
-            e_all, e_send, e_recv, e_over, minus, plus, xb, xa
-        )
+        m_first(m_ref)
         m_start(m_ref)
+        e_first(e_ref)
+        e_start(e_ref)
         copy(m_ref, place(m_all, x, y, B), m_send, m_sib, sibling).start()
         m_one()
-        e_start(e_ref)
+        e_one()
         m_two()
+        e_two()
         m_three()
-        e_one()
+        e_three()
         m_four()
-        e_two()
-        e_three()
         e_four()
 
     def h_place(cy, cz):

time: 58.2 us -> 56.7 us (0.974)
  Pallas kernels: 55.5 us -> 54.1 us
    pallas_call x1, Pallas kernels: 55.5 us -> 54.1 us  [local(): pl.pallas_call(functools.partial(kernel, nz, 3.0 / math.sqrt(width)), out...]
where the time goes in v4:
time: 56.7 us; the launch traced here: 56.6 us
  Pallas kernels  54.1 us (95%)
  local copies, waits for them, and re-layouts  1.92 us (3%)
  between operations  0.64 us (1%)
    pallas_call x1, Pallas kernels, local(): pl.pallas_call(functools.partial(kernel, nz, 3.0 / math.sqrt(width)), out...  54.1 us
    unnamed x3, local copies, waits for them, and re-layouts  1.92 us

profile of v4, /device:TPU:1, one launch (start us, length us, event | category | flops | bytes accessed | tf_op | source)
XLA Modules:
  0.0 56.6 jit_solution(10551193726943670947)
XLA Ops:
  0.6 54.1 %shard_map.58 = (f32[1,128]{1,0:T(1,128)S(1)}, bf16[128,1024]{1,0:T(8,128)(2,1)S(1)}, bf16[128,1024]{1,0:T(8,128)(2,1)S(1)}) custom-call(bf16[128,1024]{1,0:T(8,128)(2,1)} %m_ref.1, bf16[128,1024]{1,0:T(8,128)(2,1)} %e_ref.1, bf16[32,1024]{1,0:T(8,128)(2,1)} %h_ref.1), custom_call_target="tpu_custom_call" | custom-call | tf_op jit(solution)/shard_map/pallas_call | solution.py:392
  54.7 0.5 copy.9
  55.2 0.7 %copy.10 = bf16[128,1024]{1,0:T(8,128)(2,1)} copy(bf16[128,1024]{1,0:T(8,128)(2,1)S(1)} %get-tuple-element.10) | data formatting | bytes 524288
  55.9 0.7 %copy.11 = bf16[128,1024]{1,0:T(8,128)(2,1)} copy(bf16[128,1024]{1,0:T(8,128)(2,1)S(1)} %get-tuple-element.11) | data formatting | bytes 524288

commit v5 on v4

--- a/solution.py
+++ b/solution.py
@@ -13,7 +13,7 @@
 MESH = pl.DeviceIdType.MESH
 NX, NY, NC = 4, 2, 2
 RANKS = NX * NY * NC
-CHUNK = 256
+CHUNK = 512
 WIDE = 512
 BITS = 2
 NT = (((1,), (1,)), ((), ()))

time: 56.7 us -> 55.4 us (0.977)
  Pallas kernels: 54.1 us -> 52.7 us
    pallas_call x1, Pallas kernels: 54.1 us -> 52.7 us  [local(): pl.pallas_call(functools.partial(kernel, nz, 3.0 / math.sqrt(width)), out...]
where the time goes in v5:
time: 55.4 us; the launch traced here: 55.3 us
  Pallas kernels  52.7 us (95%)
  local copies, waits for them, and re-layouts  1.92 us (3%)
  between operations  0.64 us (1%)
    pallas_call x1, Pallas kernels, local(): pl.pallas_call(functools.partial(kernel, nz, 3.0 / math.sqrt(width)), out...  52.7 us
    unnamed x3, local copies, waits for them, and re-layouts  1.92 us

profile of v5, /device:TPU:1, one launch (start us, length us, event | category | flops | bytes accessed | tf_op | source)
XLA Modules:
  0.0 55.3 jit_solution(7653637139832519478)
XLA Ops:
  0.6 52.7 %shard_map.58 = (f32[1,128]{1,0:T(1,128)S(1)}, bf16[128,1024]{1,0:T(8,128)(2,1)S(1)}, bf16[128,1024]{1,0:T(8,128)(2,1)S(1)}) custom-call(bf16[128,1024]{1,0:T(8,128)(2,1)} %m_ref.1, bf16[128,1024]{1,0:T(8,128)(2,1)} %e_ref.1, bf16[32,1024]{1,0:T(8,128)(2,1)} %h_ref.1), custom_call_target="tpu_custom_call" | custom-call | tf_op jit(solution)/shard_map/pallas_call | solution.py:392
  53.4 0.5 copy.9
  53.9 0.7 %copy.10 = bf16[128,1024]{1,0:T(8,128)(2,1)} copy(bf16[128,1024]{1,0:T(8,128)(2,1)S(1)} %get-tuple-element.10) | data formatting | bytes 524288
  54.6 0.7 %copy.11 = bf16[128,1024]{1,0:T(8,128)(2,1)} copy(bf16[128,1024]{1,0:T(8,128)(2,1)S(1)} %get-tuple-element.11) | data formatting | bytes 524288
